TPU v7x, 32 devices: a whole 2x2x4 slice. The times are simulated.
32 devices in a mesh: rep: 4 (over y, core), shard: 8 (over z, x).
Axes of the slice: x: 2, y: 2, z: 4, core: 2. Of those that a mesh axis runs over, the one named last changes fastest.
Arguments:
- grad_kv: bfloat16 [4, 2, 8192, 1024], P('rep', None, 'shard'), may hold values from -24 to 24
- error_kv: float32 [4, 2, 8192, 1024], P('rep', None, 'shard'), may hold values from -12 to 12
- basis_kv: float32 [2, 1024, 64], replicated, may hold values from -6 to 6
Outputs:
- update_kv: bfloat16 [2, 8192, 1024], P(None, 'shard')
- new_error: float32 [4, 2, 8192, 1024], P('rep', None, 'shard')
- basis_next: float32 [2, 1024, 64], replicated
All inputs are finite; a program needn't handle non-finite values.
Results may differ from a plain program's by a relative error of at most 0.001.
Values sent between devices are 32-bit elements; how exact they have to be, the bound alone decides.
No kernel may reach another device: no remote copies, remote signals or barrier semaphores. Data moves between devices by JAX's collectives and lax.ppermute only.
A program may use at most 64 MiB of HBM per device.

v0:
```python
import jax
import jax.numpy as jnp
from jax import lax
from jax.sharding import PartitionSpec as P


def orthogonal(left, gram):
    chol = jnp.linalg.cholesky(gram)
    ortho = lax.linalg.triangular_solve(chol, left, left_side=False, lower=True, transpose_a=True)
    return (chol, ortho)


def on_device(grad_kv, error_kv, basis_kv):
    highest = lax.Precision.HIGHEST
    replicas = lax.axis_size("rep")
    merged = grad_kv[0].astype(jnp.float32) + error_kv[0]
    local_left = jnp.einsum("mrc,mck->mrk", merged, basis_kv, precision=highest)
    left = lax.psum(local_left, "rep") / replicas
    local_gram = jnp.einsum("mrk,mrl->mkl", left, left, precision=highest)
    gram = lax.psum(local_gram, "shard")
    chol, ortho = orthogonal(left, gram)
    local_right = jnp.einsum("mrc,mrk->mck", merged, ortho, precision=highest)
    shares = lax.psum_scatter(local_right, "shard", scatter_dimension=1, tiled=True)
    shares = lax.psum(shares, "rep")
    right = lax.all_gather(shares, "shard", axis=1, tiled=True) / replicas
    approx = jnp.einsum("mrk,mck->mrc", ortho, right, precision=highest)
    new_error = (merged - approx)[None]
    return (approx.astype(jnp.bfloat16), new_error, right)


def solution(mesh):
    placed = (P("rep", None, "shard", None), P("rep", None, "shard", None), P())
    return jax.shard_map(
        on_device,
        mesh=mesh,
        in_specs=placed,
        out_specs=(P(None, "shard", None), P("rep", None, "shard", None), P()),
        check_vma=False,
    )
```

profile of v0, /device:TPU:0, one launch (start us, length us, event | category | flops | bytes accessed | tf_op | source)
XLA Modules:
  0.0 273.9 jit_solution(2722910858909565346)
XLA Ops:
  7.2 0.0 copy-start
  7.2 0.0 all-reduce.3.cloned.1.call-start
  7.2 1.0 copy-done
  8.2 12.4 %fusion.2 = f32[2,1024,64]{1,2,0:T(8,128)} fusion(f32[2,1024,64]{1,2,0:T(8,128)S(1)} %copy-done, f32[1,2,1024,1024]{3,2,1,0:T(8,128)} %param.4, bf16[1,2,1024,1024]{3,2,1,0:T(8,128)(2,1)} %param.3), kind=kOutput, calls=%fused_computation.3 | convolution fusion | flops 1614807040 | bytes 13631488 | tf_op jit(solution)/shard_map/mrc,mck->mrk/dot_general | solution.py:17
  20.6 0.0 all-reduce.3.cloned.1.call-update
  20.6 0.0 reduce-scatter.2.cloned.1.call-start
  20.7 36.2 %all-reduce.3.cloned.1.call-done = f32[2,1024,64]{1,2,0:T(8,128)} async-done(((f32[2,1024,64]{1,2,0:T(8,128)}), f32[2,1024,64]{1,2,0:T(8,128)}) %all-reduce.3.cloned.1.call-update) | async-done | bytes 524304 | tf_op jit(solution)/shard_map/psum | solution.py:18
  56.9 1.9 fusion.7
  58.8 37.5 %psum.22 = f32[2,64,64]{1,2,0:T(8,128)S(1)} all-reduce(f32[2,64,64]{1,2,0:T(8,128)S(1)} %fusion.7), channel_id=1, replica_groups=mesh['rep'=4,'shard'=8] {'shard'}, use_global_device_ids=true, to_apply=%region_1.0 | all-reduce | flops 8192 | bytes 65536 | tf_op jit(solution)/shard_map/psum | solution.py:20
  96.3 0.1 copy.10
  96.4 11.7 %custom-call.7 = f32[2,64,64]{2,1,0:T(8,128)S(1)} custom-call(f32[2,64,64]{2,1,0:T(8,128)S(1)} %fusion.12), custom_call_target="Cholesky" | custom-call | tf_op jit(solution)/shard_map/jit(cholesky)/cholesky | solution.py:8
  108.2 0.1 compare_reduce_fusion
  108.3 0.1 select_bitcast_fusion
  108.4 9.8 %custom-call.8 = f32[2,1,64,64]{2,3,1,0:T(8,128)S(1)} custom-call(f32[2,1,64,64]{3,2,1,0:T(8,128)S(1)} %select_bitcast_fusion), custom_call_target="InvertDiagBlocksLowerTriangular" | custom-call | tf_op jit(solution)/shard_map/triangular_solve | solution.py:9
  118.2 1.7 fusion.5
  119.9 9.6 %fusion = f32[2,1024,64]{1,2,0:T(8,128)} fusion(f32[2,1024,64]{1,2,0:T(8,128)S(1)} %fusion.5, f32[1,2,1024,1024]{3,2,1,0:T(8,128)} %param.4, bf16[1,2,1024,1024]{3,2,1,0:T(8,128)(2,1)} %param.3), kind=kOutput, calls=%fused_computation.1 | convolution fusion | flops 1614807040 | bytes 13631488 | tf_op jit(solution)/shard_map/mrc,mrk->mck/dot_general | solution.py:22
  129.6 0.0 reduce-scatter.2.cloned.1.call-update
  129.6 0.0 all-reduce.5.cloned.1.call-start
  129.6 59.7 %reduce-scatter.2.cloned.1.call-done = f32[2,128,64]{1,2,0:T(8,128)} async-done(((f32[2,1024,64]{1,2,0:T(8,128)}), f32[2,128,64]{1,2,0:T(8,128)}) %reduce-scatter.2.cloned.1.call-update) | async-done | bytes 65552 | tf_op jit(solution)/shard_map/reduce_scatter | solution.py:23
  189.4 0.0 all-reduce.5.cloned.1.call-update
  189.4 32.9 %all-reduce.5.cloned.1.call-done = f32[2,128,64]{1,2,0:T(8,128)} async-done(((f32[2,128,64]{1,2,0:T(8,128)}), f32[2,128,64]{1,2,0:T(8,128)}) %all-reduce.5.cloned.1.call-update) | async-done | bytes 65552 | tf_op jit(solution)/shard_map/psum | solution.py:24
  222.3 31.8 %all_gather.3 = f32[2,1024,64]{1,2,0:T(8,128)S(1)} all-gather(f32[2,128,64]{1,2,0:T(8,128)} %all-reduce.5.cloned.1.call-done), channel_id=1, replica_groups=mesh['rep'=4,'shard'=8] {'shard'}, dimensions={1}, use_global_device_ids=true | all-gather | bytes 589824 | tf_op jit(solution)/shard_map/all_gather | solution.py:25
  254.1 0.0 copy-start.1
  254.1 13.3 %fusion.4 = (f32[1,2,1024,1024]{3,2,1,0:T(8,128)}, bf16[2,1024,1024]{2,1,0:T(8,128)(2,1)}) fusion(f32[1,2,1024,1024]{3,2,1,0:T(8,128)} %param.4, bf16[1,2,1024,1024]{3,2,1,0:T(8,128)(2,1)} %param.3, f32[2,1024,64]{1,2,0:T(8,128)S(1)} %fusion.5, f32[2,1024,64]{1,2,0:T(8,128)S(1)} %broadcast_multiply_fusion), kind=kOutput, calls=%fused_computation.5 | convolution fusion | flops 1619001344 | bytes 26214400 | tf_op jit(solution)/shard_map/mrk,mck->mrc/dot_general | solution.py:26
  267.4 0.0 copy-done.1
  (5 shorter events, 0.1 us)
Async XLA Ops:
  7.2 1.0 copy-start
  7.2 49.8 %all-reduce.3.cloned.1.call-start = ((), (), s32[]{:S(2)}) async-start(), calls=%async_computation.1 | async-start | bytes 1048576 | tf_op jit(solution)/shard_map/psum | solution.py:18
  20.6 168.7 %reduce-scatter.2.cloned.1.call-start = ((), (), s32[]{:S(2)}) async-start(), calls=%async_computation.2 | async-start | bytes 589824 | tf_op jit(solution)/shard_map/reduce_scatter | solution.py:23
  129.6 92.7 %all-reduce.5.cloned.1.call-start = ((), (), s32[]{:S(2)}) async-start(), calls=%async_computation.3 | async-start | bytes 131072 | tf_op jit(solution)/shard_map/psum | solution.py:24
  254.1 13.3 %copy-start.1 = (f32[2,1024,64]{1,2,0:T(8,128)}, f32[2,1024,64]{1,2,0:T(8,128)S(1)}, u32[]{:S(2)}) copy-start(f32[2,1024,64]{1,2,0:T(8,128)S(1)} %broadcast_multiply_fusion) | copy-start | bytes 1572868
Sparse Core Ops, SparseCore 0:
  20.8 36.1 all-reduce.2
  129.7 59.6 reduce-scatter.1
  191.7 30.5 all-reduce.4
where the time goes:
time: 274 us
  waiting for transfers between devices  129 us (47%)
  blocking collectives  69.3 us (25%)
  matrix products  38.9 us (14%)
  other arithmetic  21.9 us (8%)
  between operations  13.8 us (5%)
    reduce_scatter x1, waiting for transfers between devices, on_device(): lax.psum_scatter(local_right, 'shard', scatter_dimension=1, tiled=True)  59.7 us
    psum x1, blocking collectives, on_device(): gram = lax.psum(local_gram, 'shard')  37.5 us
    psum x1, waiting for transfers between devices, on_device(): left = lax.psum(local_left, 'rep') / replicas  36.2 us
    psum x1, waiting for transfers between devices, on_device(): shares = lax.psum(shares, 'rep')  32.9 us
    all_gather x1, blocking collectives, on_device(): right = lax.all_gather(shares, 'shard', axis=1, tiled=True) / replicas  31.8 us
    dot_general x1, matrix products, on_device(): approx = jnp.einsum('mrk,mck->mrc', ortho, right, precision=highest)  13.3 us
    dot_general x1, matrix products, on_device(): local_left = jnp.einsum('mrc,mck->mrk', merged, basis_kv, precision=highest)  12.4 us
    another operation x4, other arithmetic, orthogonal(): chol = jnp.linalg.cholesky(gram)  11.9 us
  transfers between devices with their start and end apart: 3, of which 3 were waited for; matrix products, arithmetic and copies ran while one was open for 0% of the time, Pallas kernels for 0%

commit v1 on v0

--- a/solution.py
+++ b/solution.py
@@ -2,6 +2,14 @@
 import jax.numpy as jnp
 from jax import lax
 from jax.sharding import PartitionSpec as P
+
+
+def sum_by_hops(block, mesh_axis):
+    size, total = (lax.axis_size(mesh_axis), block)
+    for far in [1 << k for k in range(size.bit_length() - 1)]:
+        swap = [(i, i ^ far) for i in range(size)]
+        total = total + lax.ppermute(total, mesh_axis, swap)
+    return total
 
 
 def orthogonal(left, gram):
@@ -17,7 +25,7 @@
     local_left = jnp.einsum("mrc,mck->mrk", merged, basis_kv, precision=highest)
     left = lax.psum(local_left, "rep") / replicas
     local_gram = jnp.einsum("mrk,mrl->mkl", left, left, precision=highest)
-    gram = lax.psum(local_gram, "shard")
+    gram = sum_by_hops(local_gram, "shard")
     chol, ortho = orthogonal(left, gram)
     local_right = jnp.einsum("mrc,mrk->mck", merged, ortho, precision=highest)
     shares = lax.psum_scatter(local_right, "shard", scatter_dimension=1, tiled=True)

time: 274 us -> 255 us (0.931)
  blocking collectives: 69.3 us -> 31.8 us
  waiting for transfers between devices: 129 us -> 141 us
  starting transfers between devices: 0.12 us -> 6.3 us
    psum x1 -> x0, blocking collectives: 37.5 us -> none  [on_device(): gram = lax.psum(local_gram, 'shard')]
    ppermute x0 -> x3, waiting for transfers between devices: none -> 7.81 us  [sum_by_hops(): total = total + lax.ppermute(total, mesh_axis, swap)]
    ppermute x0 -> x3, starting transfers between devices: none -> 6.18 us  [sum_by_hops(): total = total + lax.ppermute(total, mesh_axis, swap)]
    reduce_scatter x1, waiting for transfers between devices: 59.7 us -> 64 us  [on_device(): lax.psum_scatter(local_right, 'shard', scatter_dimension=1, tiled=True)]
  transfers between devices with their start and end apart: 3 -> 6, of which waited for: 3 -> 6; matrix products, arithmetic and copies ran while one was open for 0% -> 0% of each run, Pallas kernels for 0% -> 0%
where the time goes in v1:
time: 255 us
  waiting for transfers between devices  141 us (55%)
  matrix products  38.9 us (15%)
  blocking collectives  31.8 us (12%)
  other arithmetic  21.9 us (9%)
  between operations  13.8 us (5%)
  starting transfers between devices  6.3 us (2%)
    reduce_scatter x1, waiting for transfers between devices, on_device(): lax.psum_scatter(local_right, 'shard', scatter_dimension=1, tiled=True)  64 us
    psum x1, waiting for transfers between devices, on_device(): left = lax.psum(local_left, 'rep') / replicas  36.3 us
    psum x1, waiting for transfers between devices, on_device(): shares = lax.psum(shares, 'rep')  32.8 us
    all_gather x1, blocking collectives, on_device(): right = lax.all_gather(shares, 'shard', axis=1, tiled=True) / replicas  31.8 us
    dot_general x1, matrix products, on_device(): approx = jnp.einsum('mrk,mck->mrc', ortho, right, precision=highest)  13.3 us
    dot_general x1, matrix products, on_device(): local_left = jnp.einsum('mrc,mck->mrk', merged, basis_kv, precision=highest)  12.4 us
    another operation x4, other arithmetic, orthogonal(): chol = jnp.linalg.cholesky(gram)  11.9 us
    another operation x3, other arithmetic, orthogonal(): lax.linalg.triangular_solve(chol, left, left_side=False, lower=True, tran...  9.92 us
  transfers between devices with their start and end apart: 6, of which 6 were waited for; matrix products, arithmetic and copies ran while one was open for 0% of the time, Pallas kernels for 0%

profile of v1, /device:TPU:0, one launch (start us, length us, event | category | flops | bytes accessed | tf_op | source)
XLA Modules:
  0.0 254.7 jit_solution(3730519452871555994)
XLA Ops:
  7.2 0.0 copy-start
  7.2 0.0 all-reduce.3.cloned.1.call-start
  7.2 1.0 copy-done
  8.2 12.4 %fusion.2 = f32[2,1024,64]{1,2,0:T(8,128)} fusion(f32[2,1024,64]{1,2,0:T(8,128)S(1)} %copy-done, f32[1,2,1024,1024]{3,2,1,0:T(8,128)} %param.4, bf16[1,2,1024,1024]{3,2,1,0:T(8,128)(2,1)} %param.3), kind=kOutput, calls=%fused_computation.3 | convolution fusion | flops 1614807040 | bytes 13631488 | tf_op jit(solution)/shard_map/mrc,mck->mrk/dot_general | solution.py:25
  20.6 0.0 all-reduce.3.cloned.1.call-update
  20.6 0.0 reduce-scatter.2.cloned.1.call-start
  20.7 36.3 %all-reduce.3.cloned.1.call-done = f32[2,1024,64]{1,2,0:T(8,128)} async-done(((f32[2,1024,64]{1,2,0:T(8,128)}), f32[2,1024,64]{1,2,0:T(8,128)}) %all-reduce.3.cloned.1.call-update) | async-done | bytes 524304 | tf_op jit(solution)/shard_map/psum | solution.py:26
  56.9 1.9 fusion.7
  58.8 1.5 collective-permute-start
  60.3 2.8 %collective-permute-done = f32[2,64,64]{1,2,0:T(8,128)S(1)} collective-permute-done((f32[2,64,64]{1,2,0:T(8,128)S(1)}, f32[2,64,64]{1,2,0:T(8,128)S(1)}, u32[]{:S(2)}, u32[]{:S(2)}) %collective-permute-start) | collective-permute-done | bytes 32800 | tf_op jit(solution)/shard_map/ppermute | solution.py:11
  63.2 1.6 collective-permute-start.1
  64.7 2.8 %collective-permute-done.1 = f32[2,64,64]{1,2,0:T(8,128)S(1)} collective-permute-done((f32[2,64,64]{1,2,0:T(8,128)S(1)}, f32[2,64,64]{1,2,0:T(8,128)S(1)}, u32[]{:S(2)}, u32[]{:S(2)}) %collective-permute-start.1) | collective-permute-done | bytes 32800 | tf_op jit(solution)/shard_map/ppermute | solution.py:11
  67.5 3.1 %collective-permute-start.2 = (f32[2,64,64]{1,2,0:T(8,128)S(1)}, f32[2,64,64]{1,2,0:T(8,128)S(1)}, u32[]{:S(2)}, u32[]{:S(2)}) collective-permute-start(f32[2,64,64]{1,2,0:T(8,128)S(1)} %add.35), channel_id=1, source_target_pairs={{0,4},{1,5},{2,6},{3,7},{4,0},{5,1},{6,2},{7,3},{8,12},{9,13},{10,... | collective-permute-start | bytes 98312 | tf_op jit(solution)/shard_map/ppermute | solution.py:11
  70.6 2.2 collective-permute-done.2
  72.9 0.1 copy.12
  73.0 11.7 %custom-call.7 = f32[2,64,64]{2,1,0:T(8,128)S(1)} custom-call(f32[2,64,64]{2,1,0:T(8,128)S(1)} %fusion.12), custom_call_target="Cholesky" | custom-call | tf_op jit(solution)/shard_map/jit(cholesky)/cholesky | solution.py:16
  84.7 0.1 compare_reduce_fusion
  84.9 0.1 select_bitcast_fusion
  84.9 9.8 %custom-call.8 = f32[2,1,64,64]{2,3,1,0:T(8,128)S(1)} custom-call(f32[2,1,64,64]{3,2,1,0:T(8,128)S(1)} %select_bitcast_fusion), custom_call_target="InvertDiagBlocksLowerTriangular" | custom-call | tf_op jit(solution)/shard_map/triangular_solve | solution.py:17
  94.8 1.7 fusion.5
  96.4 9.6 %fusion = f32[2,1024,64]{1,2,0:T(8,128)} fusion(f32[2,1024,64]{1,2,0:T(8,128)S(1)} %fusion.5, f32[1,2,1024,1024]{3,2,1,0:T(8,128)} %param.4, bf16[1,2,1024,1024]{3,2,1,0:T(8,128)(2,1)} %param.3), kind=kOutput, calls=%fused_computation.1 | convolution fusion | flops 1614807040 | bytes 13631488 | tf_op jit(solution)/shard_map/mrc,mrk->mck/dot_general | solution.py:30
  106.1 0.0 reduce-scatter.2.cloned.1.call-update
  106.1 0.0 all-reduce.5.cloned.1.call-start
  106.2 64.0 %reduce-scatter.2.cloned.1.call-done = f32[2,128,64]{1,2,0:T(8,128)} async-done(((f32[2,1024,64]{1,2,0:T(8,128)}), f32[2,128,64]{1,2,0:T(8,128)}) %reduce-scatter.2.cloned.1.call-update) | async-done | bytes 65552 | tf_op jit(solution)/shard_map/reduce_scatter | solution.py:31
  170.2 0.0 all-reduce.5.cloned.1.call-update
  170.2 32.8 %all-reduce.5.cloned.1.call-done = f32[2,128,64]{1,2,0:T(8,128)} async-done(((f32[2,128,64]{1,2,0:T(8,128)}), f32[2,128,64]{1,2,0:T(8,128)}) %all-reduce.5.cloned.1.call-update) | async-done | bytes 65552 | tf_op jit(solution)/shard_map/psum | solution.py:32
  203.0 31.8 %all_gather.3 = f32[2,1024,64]{1,2,0:T(8,128)S(1)} all-gather(f32[2,128,64]{1,2,0:T(8,128)} %all-reduce.5.cloned.1.call-done), channel_id=1, replica_groups=mesh['rep'=4,'shard'=8] {'shard'}, dimensions={1}, use_global_device_ids=true | all-gather | bytes 589824 | tf_op jit(solution)/shard_map/all_gather | solution.py:33
  234.9 0.0 copy-start.1
  234.9 13.3 %fusion.4 = (f32[1,2,1024,1024]{3,2,1,0:T(8,128)}, bf16[2,1024,1024]{2,1,0:T(8,128)(2,1)}) fusion(f32[1,2,1024,1024]{3,2,1,0:T(8,128)} %param.4, bf16[1,2,1024,1024]{3,2,1,0:T(8,128)(2,1)} %param.3, f32[2,1024,64]{1,2,0:T(8,128)S(1)} %fusion.5, f32[2,1024,64]{1,2,0:T(8,128)S(1)} %broadcast_multiply_fusion), kind=kOutput, calls=%fused_computation.5 | convolution fusion | flops 1619001344 | bytes 26214400 | tf_op jit(solution)/shard_map/mrk,mck->mrc/dot_general | solution.py:34
  248.2 0.0 copy-done.1
  (8 shorter events, 0.1 us)
Async XLA Ops:
  7.2 1.0 copy-start
  7.2 49.8 %all-reduce.3.cloned.1.call-start = ((), (), s32[]{:S(2)}) async-start(), calls=%async_computation.1 | async-start | bytes 1048576 | tf_op jit(solution)/shard_map/psum | solution.py:26
  20.6 149.5 %reduce-scatter.2.cloned.1.call-start = ((), (), s32[]{:S(2)}) async-start(), calls=%async_computation.2 | async-start | bytes 589824 | tf_op jit(solution)/shard_map/reduce_scatter | solution.py:31
  58.8 4.3 %collective-permute-start = (f32[2,64,64]{1,2,0:T(8,128)S(1)}, f32[2,64,64]{1,2,0:T(8,128)S(1)}, u32[]{:S(2)}, u32[]{:S(2)}) collective-permute-start(f32[2,64,64]{1,2,0:T(8,128)S(1)} %fusion.7), channel_id=1, source_target_pairs={{0,1},{1,0},{2,3},{3,2},{4,5},{5,4},{6,7},{7,6},{8,9},{9,8},{10,11... | collective-permute-start | bytes 98312 | tf_op jit(solution)/shard_map/ppermute | solution.py:11
  63.2 4.3 %collective-permute-start.1 = (f32[2,64,64]{1,2,0:T(8,128)S(1)}, f32[2,64,64]{1,2,0:T(8,128)S(1)}, u32[]{:S(2)}, u32[]{:S(2)}) collective-permute-start(f32[2,64,64]{1,2,0:T(8,128)S(1)} %add.34), channel_id=1, source_target_pairs={{0,2},{1,3},{2,0},{3,1},{4,6},{5,7},{6,4},{7,5},{8,10},{9,11},{10,... | collective-permute-start | bytes 98312 | tf_op jit(solution)/shard_map/ppermute | solution.py:11
  67.5 5.3 %collective-permute-start.2 = (f32[2,64,64]{1,2,0:T(8,128)S(1)}, f32[2,64,64]{1,2,0:T(8,128)S(1)}, u32[]{:S(2)}, u32[]{:S(2)}) collective-permute-start(f32[2,64,64]{1,2,0:T(8,128)S(1)} %add.35), channel_id=1, source_target_pairs={{0,4},{1,5},{2,6},{3,7},{4,0},{5,1},{6,2},{7,3},{8,12},{9,13},{10,... | collective-permute-start | bytes 98312 | tf_op jit(solution)/shard_map/ppermute | solution.py:11
  106.1 96.9 %all-reduce.5.cloned.1.call-start = ((), (), s32[]{:S(2)}) async-start(), calls=%async_computation.3 | async-start | bytes 131072 | tf_op jit(solution)/shard_map/psum | solution.py:32
  234.9 13.3 %copy-start.1 = (f32[2,1024,64]{1,2,0:T(8,128)}, f32[2,1024,64]{1,2,0:T(8,128)S(1)}, u32[]{:S(2)}) copy-start(f32[2,1024,64]{1,2,0:T(8,128)S(1)} %broadcast_multiply_fusion) | copy-start | bytes 1572868
Sparse Core Ops, SparseCore 0:
  20.8 36.1 all-reduce.2
  106.2 63.8 reduce-scatter.1
  172.5 30.5 all-reduce.4
